TPU v7x, 128 devices: a whole 4x4x4 slice. The times are simulated.
128 devices in a mesh: dom: 128 (over x, z, y, core).
Axes of the slice: x: 4, y: 4, z: 4, core: 2. Of those that a mesh axis runs over, the one named last changes fastest.
Arguments:
- features: bfloat16 [262144, 512], P('dom'), may hold values from -6 to 6
- weight: bfloat16 [512, 512], replicated, may hold values from -0.25 to 0.25
- cotangent: bfloat16 [262144, 512], P('dom'), may hold values from -6 to 6
- tile_values: bfloat16 [12288, 128, 128], P('dom'), may hold values from -0.21875 to 0.21875
- tile_rows: int32 [12288], P('dom'), may hold values from 0 to 15
- tile_cols: int32 [12288], P('dom'), may hold values from 0 to 27, as said below
- hub_rows: int32 [512], P('dom'), may hold values from 0 to 2047
- send_rows: int32 [128, 128, 8], P('dom'), may hold values from 0 to 2047
- send_count: int32 [128, 128], P('dom'), may hold values from 1 to 8, as said below
Outputs:
- output: bfloat16 [262144, 512], P('dom')
- grad_features: bfloat16 [262144, 512], P('dom')
- grad_weight: float32 [512, 512], replicated
Inputs may be any that keep to these rules, and one draw needn't show every extreme that they name: `tile_cols`: on every device the first 64 tiles name column blocks below 20 and the other 32 name blocks from 20 on. `send_count`: every source sends 8 rows to at least one device.
All inputs are finite; a program needn't handle non-finite values.
Results may differ from a plain program's by a relative error of at most 0.019.
Values may be sent and summed in bfloat16 or wider, within the bound.
A program may use at most 128 MiB of HBM per device.

v0:
```python
import math
import jax
import jax.numpy as jnp
from jax import lax
from jax.sharding import PartitionSpec as P

LOC_TILES = 64


def one_hot(index, count):
    return (index[:, None] == jnp.arange(count, dtype=jnp.int32)[None, :]).astype(jnp.bfloat16)


def pick_blocks(index, blocks):
    selector = one_hot(index, blocks.shape[0])
    return jnp.einsum("kc,cjf->kjf", selector, blocks, preferred_element_type=jnp.float32).astype(
        blocks.dtype
    )


def add_into(selector, terms):
    upper = terms.astype(jnp.bfloat16)
    lower = (terms - upper.astype(jnp.float32)).astype(jnp.bfloat16)
    first = jnp.einsum("kr,kif->rif", selector, upper, preferred_element_type=jnp.float32)
    return first + jnp.einsum("kr,kif->rif", selector, lower, preferred_element_type=jnp.float32)


def apply_tiles(values, row_idx, col_idx, table_blocks, running):
    tile_count, tile_size = (values.shape[0], values.shape[1])
    group_size = math.gcd(tile_count, 32)
    row_count = running.shape[0]

    def apply_advance(carry, packed):
        vals_group, rows_group, cols_group = packed
        picked = pick_blocks(cols_group, table_blocks)
        products = jnp.einsum(
            "kij,kjf->kif", vals_group, picked, preferred_element_type=jnp.float32
        )
        return (carry + add_into(one_hot(rows_group, row_count), products), None)

    packed = (
        values.reshape(-1, group_size, tile_size, tile_size),
        row_idx.reshape(-1, group_size),
        col_idx.reshape(-1, group_size),
    )
    result, _ = lax.scan(apply_advance, running, packed)
    return result


def spread_tiles(values, row_idx, col_idx, grad_blocks, running):
    tile_count, tile_size = (values.shape[0], values.shape[1])
    group_size = math.gcd(tile_count, 32)
    col_count = running.shape[0]

    def spread_advance(carry, packed):
        vals_group, rows_group, cols_group = packed
        picked = pick_blocks(rows_group, grad_blocks)
        products = jnp.einsum(
            "kij,kif->kjf", vals_group, picked, preferred_element_type=jnp.float32
        )
        return (carry + add_into(one_hot(cols_group, col_count), products), None)

    packed = (
        values.reshape(-1, group_size, tile_size, tile_size),
        row_idx.reshape(-1, group_size),
        col_idx.reshape(-1, group_size),
    )
    result, _ = lax.scan(spread_advance, running, packed)
    return result


def per_device(
    features, weight, cotangent, tile_values, tile_rows, tile_cols, hub_rows, send_rows, send_count
):
    num_dev = lax.axis_size("dom")
    row_count, feat_width = features.shape
    tile_size = tile_values.shape[1]
    row_blocks = row_count // tile_size
    slot_count = send_rows.shape[2]
    split_at = LOC_TILES
    hub_select = one_hot(hub_rows, row_count)
    hub_local = jnp.dot(hub_select, features, preferred_element_type=jnp.float32).astype(
        jnp.bfloat16
    )
    hub_all = lax.all_gather(hub_local, "dom", axis=0, tiled=True)
    targets = send_rows[0]
    counts = send_count[0]
    live_slots = jnp.arange(slot_count, dtype=jnp.int32)[None, :] < counts[:, None]
    target_select = one_hot(targets.reshape(-1), row_count) * live_slots.reshape(-1, 1).astype(
        jnp.bfloat16
    )
    outgoing = (
        jnp.dot(target_select, features, preferred_element_type=jnp.float32)
        .astype(jnp.bfloat16)
        .reshape(num_dev, slot_count, feat_width)
    )
    incoming = lax.all_to_all(outgoing, "dom", split_axis=0, concat_axis=0, tiled=True)
    near_table = jnp.concatenate([features, hub_all], axis=0).reshape(-1, tile_size, feat_width)
    far_table = incoming.reshape(-1, tile_size, feat_width)
    near_blocks = near_table.shape[0]
    empty = jnp.zeros((row_blocks, tile_size, feat_width), jnp.float32)
    summed = apply_tiles(
        tile_values[:split_at], tile_rows[:split_at], tile_cols[:split_at], near_table, empty
    )
    summed = apply_tiles(
        tile_values[split_at:],
        tile_rows[split_at:],
        tile_cols[split_at:] - near_blocks,
        far_table,
        summed,
    )
    aggregated = summed.reshape(row_count, feat_width).astype(jnp.bfloat16)
    pre_act = jnp.dot(aggregated, weight, preferred_element_type=jnp.float32)
    sigmoid_pre = jax.nn.sigmoid(pre_act)
    output = (pre_act * sigmoid_pre).astype(jnp.bfloat16)
    grad_pre = (
        cotangent.astype(jnp.float32) * sigmoid_pre * (1.0 + pre_act * (1.0 - sigmoid_pre))
    ).astype(jnp.bfloat16)
    weight_term = lax.dot_general(
        aggregated, grad_pre, (((0,), (0,)), ((), ())), preferred_element_type=jnp.float32
    )
    weight_term = weight_term * float(row_count * num_dev) ** (-0.5)
    grad_weight = lax.psum(weight_term, "dom")
    grad_agg = lax.dot_general(
        grad_pre, weight, (((1,), (1,)), ((), ())), preferred_element_type=jnp.float32
    ).astype(jnp.bfloat16)
    grad_blocks = grad_agg.reshape(row_blocks, tile_size, feat_width)
    near_grad = spread_tiles(
        tile_values[:split_at],
        tile_rows[:split_at],
        tile_cols[:split_at],
        grad_blocks,
        jnp.zeros((near_blocks, tile_size, feat_width), jnp.float32),
    )
    far_grad = spread_tiles(
        tile_values[split_at:],
        tile_rows[split_at:],
        tile_cols[split_at:] - near_blocks,
        grad_blocks,
        jnp.zeros((far_table.shape[0], tile_size, feat_width), jnp.float32),
    )
    near_flat = near_grad.reshape(-1, feat_width)
    own_grad = near_flat[:row_count]
    hub_grad = near_flat[row_count:]
    far_flat = far_grad.reshape(num_dev, slot_count, feat_width)
    hub_mine = lax.psum_scatter(hub_grad, "dom", scatter_dimension=0, tiled=True)
    returned = lax.all_to_all(
        far_flat.astype(jnp.bfloat16), "dom", split_axis=0, concat_axis=0, tiled=True
    ).astype(far_flat.dtype)
    hub_part = add_into(hub_select, hub_mine[:, None, :])[:, 0, :]
    halo_part = add_into(target_select, returned.reshape(-1, 1, feat_width))[:, 0, :]
    grad_features = own_grad + hub_part + halo_part
    return (output, grad_features.astype(jnp.bfloat16), grad_weight)


def solution(mesh):
    placed = (
        P("dom", None),
        P(),
        P("dom", None),
        P("dom", None, None),
        P("dom"),
        P("dom"),
        P("dom"),
        P("dom", None, None),
        P("dom", None),
    )
    return jax.shard_map(
        per_device,
        mesh=mesh,
        in_specs=placed,
        out_specs=(P("dom", None), P("dom", None), P()),
        check_vma=False,
    )
```

profile of v0, /device:TPU:1, one launch (start us, length us, event | category | flops | bytes accessed | tf_op | source)
XLA Modules:
  0.0 434.4 jit_solution(5442505142722184858)
XLA Ops:
  9.6 4.9 %fusion.69 = bf16[128,8,512]{2,1,0:T(8,128)(2,1)} fusion(bf16[2048,512]{1,0:T(8,128)(2,1)} %param.13, s32[1024]{0:T(1024)S(1)} %eq.165, bf16[1024]{0:T(1024)(128)(2,1)S(1)} %reshape.143), kind=kOutput, calls=%fused_computation.85 | convolution fusion | flops 2152202240 | bytes 3151872 | tf_op jit(solution)/shard_map/dot_general | solution.py:93
  14.5 12.0 %all-to-all-start = ((bf16[128,8,512]{2,1,0:T(8,128)(2,1)}), bf16[128,8,512]{2,1,0:T(8,128)(2,1)}, u32[]{:S(2)}, u32[]{:S(2)}) async-start(bf16[128,8,512]{2,1,0:T(8,128)(2,1)} %fusion.69), calls=%async_computation | async-start | bytes 2097152 | tf_op jit(solution)/shard_map/all_to_all | solution.py:97
  27.1 45.4 %all-gather = bf16[128,4,512]{2,1,0:T(4,128)(2,1)} all-gather(bf16[1,4,512]{2,1,0:T(4,128)(2,1)S(1)} %fusion.72), channel_id=1, replica_groups=mesh['dom'=128] {'dom'}, dimensions={0}, use_global_device_ids=true | all-gather | bytes 528384 | tf_op jit(solution)/shard_map/all_gather | solution.py:85
  77.0 42.9 %while.6 = (s32[]{:T(128)}, f32[16,128,512]{2,0,1:T(8,128)}, s32[2,32]{1,0:T(2,128)S(1)}, bf16[2,32,128,128]{3,2,1,0:T(8,128)(2,1)S(1)}, s32[2,32]{1,0:T(2,128)S...) while((s32[]{:T(128)}, f32[16,128,512]{2,0,1:T(8,128)}, s32[2,32]{1,0:T(2,128)S(1)}, ...), condition=%wide.region_1.2_spmd.clone, body=%wide.region_0.1_spmd.clone.sunk | while | flops 768607872 | bytes 45614052 | solution.py:46
  84.4 4.8 %fusion.142 = f32[16,128,512]{2,0,1:T(8,128)} fusion(bf16[32,128,512]{2,1,0:T(8,128)(2,1)S(1)} %get-tuple-element.300, s32[32]{0:T(128)S(1)} %get-tuple-element.301), kind=kOutput, calls=%fused_computation.1.clone.1 | convolution fusion | flops 67109376 | bytes 8388736 | tf_op jit(solution)/shard_map/while/body/eval_jaxpr/kr,kif->rif/dot_general | solution.py:25
  89.2 8.6 %select_add_fusion.4 = f32[16,128,512]{2,0,1:T(8,128)} fusion(f32[16,128,512]{2,0,1:T(8,128)} %get-tuple-element.322, f32[16,128,512]{2,0,1:T(8,128)} %fusion.142, bf16[32,128,512]{2,1,0:T(8,128)(2,1)} %get-tuple-element.302, pred[]{:T(512)S(6)} %compare.6, s32[32]{0:T(128)S(1)} %get-tuple-element.301), kind=kOutput, calls=%fused_computation.7.clone.1 | convolution fusion | flops 70255104 | bytes 16777344 | tf_op jit(solution)/shard_map/while/body/eval_jaxpr/kr,kif->rif/dot_general | solution.py:24
  110.1 9.8 %select_add_fusion.4 = f32[16,128,512]{2,0,1:T(8,128)} fusion(f32[16,128,512]{2,0,1:T(8,128)} %get-tuple-element.322, f32[16,128,512]{2,0,1:T(8,128)} %fusion.142, bf16[32,128,512]{2,1,0:T(8,128)(2,1)} %get-tuple-element.302, pred[]{:T(512)S(6)} %compare.6, s32[32]{0:T(128)S(1)} %get-tuple-element.301), kind=kOutput, calls=%fused_computation.7.clone.1 | convolution fusion | flops 70255104 | bytes 16777344 | tf_op jit(solution)/shard_map/while/body/eval_jaxpr/kr,kif->rif/dot_general | solution.py:24
  126.0 8.7 %fusion.43 = (bf16[32,128,512]{1,2,0:T(8,128)(2,1)}, bf16[32,128,512]{1,2,0:T(8,128)(2,1)}) fusion(bf16[96,128,128]{2,1,0:T(8,128)(2,1)S(1)} %copy-done.4, bf16[32,128,512]{2,0,1:T(8,128)(2,1)S(1)} %convolution_convert_fusion.3), kind=kOutput, calls=%fused_computation.51 | convolution fusion | flops 545259520 | bytes 13631488 | tf_op jit(solution)/shard_map/while/body/eval_jaxpr/kij,kjf->kif/dot_general | solution.py:36
  134.7 8.0 %copy.71 = bf16[32,128,512]{2,0,1:T(8,128)(2,1)} copy(bf16[32,128,512]{1,2,0:T(8,128)(2,1)} %get-tuple-element.216) | data formatting | bytes 8388608 | tf_op jit(solution)/shard_map/while/body/eval_jaxpr/convert_element_type | solution.py:22
  142.7 7.9 %copy.72 = bf16[32,128,512]{2,0,1:T(8,128)(2,1)} copy(bf16[32,128,512]{1,2,0:T(8,128)(2,1)} %get-tuple-element.215) | data formatting | bytes 8388608 | tf_op jit(solution)/shard_map/while/body/eval_jaxpr/convert_element_type | solution.py:23
  166.2 8.8 %fusion.42 = (bf16[32,128,512]{1,2,0:T(8,128)(2,1)}, bf16[32,128,512]{1,2,0:T(8,128)(2,1)}) fusion(bf16[96,128,128]{2,1,0:T(8,128)(2,1)S(1)} %copy-done.5, bf16[32,128,512]{2,0,1:T(8,128)(2,1)S(1)} %convolution_convert_fusion.4), kind=kOutput, calls=%fused_computation.48 | convolution fusion | flops 545259520 | bytes 13631488 | tf_op jit(solution)/shard_map/while/body/eval_jaxpr/kij,kif->kjf/dot_general | solution.py:58
  175.0 7.9 %copy.79 = bf16[32,128,512]{2,0,1:T(8,128)(2,1)} copy(bf16[32,128,512]{1,2,0:T(8,128)(2,1)} %get-tuple-element.214) | data formatting | bytes 8388608 | tf_op jit(solution)/shard_map/while/body/eval_jaxpr/convert_element_type | solution.py:22
  187.1 7.9 %copy.80 = bf16[32,128,512]{2,0,1:T(8,128)(2,1)} copy(bf16[32,128,512]{1,2,0:T(8,128)(2,1)} %get-tuple-element.213) | data formatting | bytes 8388608 | tf_op jit(solution)/shard_map/while/body/eval_jaxpr/convert_element_type | solution.py:23
  199.9 4.9 %all-to-all-start.1 = ((bf16[128,8,512]{2,1,0:T(8,128)(2,1)}), bf16[128,8,512]{2,1,0:T(8,128)(2,1)}, u32[]{:S(2)}, u32[]{:S(2)}) async-start(bf16[128,8,512]{2,1,0:T(8,128)(2,1)} %bitcast.126), calls=%async_computation.1 | async-start | bytes 2097152 | tf_op jit(solution)/shard_map/all_to_all | solution.py:147
  204.8 46.0 %while.7 = (s32[]{:T(128)}, f32[20,128,512]{2,0,1:T(8,128)}, s32[2,32]{1,0:T(2,128)S(1)}, bf16[2,32,128,128]{2,3,1,0:T(8,128)(2,1)}, s32[2,32]{1,0:T(2,128)S(1)}...) while((s32[]{:T(128)}, f32[20,128,512]{2,0,1:T(8,128)}, s32[2,32]{1,0:T(2,128)S(1)}, ...), condition=%wide.region_3.4_spmd.clone, body=%wide.region_2.3_spmd.clone.sunk | while | flops 786171648 | bytes 57672704 | solution.py:68
  210.6 5.8 %fusion.150 = f32[20,128,512]{2,0,1:T(8,128)} fusion(bf16[32,128,512]{2,1,0:T(8,128)(2,1)S(1)} %get-tuple-element.310, s32[32]{0:T(128)S(1)} %get-tuple-element.311), kind=kOutput, calls=%fused_computation.25.clone.1 | convolution fusion | flops 83886720 | bytes 9437312 | tf_op jit(solution)/shard_map/while/body/eval_jaxpr/kr,kif->rif/dot_general | solution.py:25
  216.4 10.4 %select_add_fusion.5 = f32[20,128,512]{2,0,1:T(8,128)} fusion(f32[20,128,512]{2,0,1:T(8,128)} %get-tuple-element.346, f32[20,128,512]{2,0,1:T(8,128)} %fusion.150, pred[]{:T(512)S(6)} %compare.7, bf16[32,128,512]{2,1,0:T(8,128)(2,1)} %get-tuple-element.312, s32[32]{0:T(128)S(1)} %get-tuple-element.311), kind=kOutput, calls=%fused_computation.24.clone.1 | convolution fusion | flops 87818880 | bytes 19923072 | tf_op jit(solution)/shard_map/while/body/eval_jaxpr/kr,kif->rif/dot_general | solution.py:24
  232.6 5.8 %fusion.150 = f32[20,128,512]{2,0,1:T(8,128)} fusion(bf16[32,128,512]{2,1,0:T(8,128)(2,1)S(1)} %get-tuple-element.310, s32[32]{0:T(128)S(1)} %get-tuple-element.311), kind=kOutput, calls=%fused_computation.25.clone.1 | convolution fusion | flops 83886720 | bytes 9437312 | tf_op jit(solution)/shard_map/while/body/eval_jaxpr/kr,kif->rif/dot_general | solution.py:25
  238.4 12.2 %select_add_fusion.5 = f32[20,128,512]{2,0,1:T(8,128)} fusion(f32[20,128,512]{2,0,1:T(8,128)} %get-tuple-element.346, f32[20,128,512]{2,0,1:T(8,128)} %fusion.150, pred[]{:T(512)S(6)} %compare.7, bf16[32,128,512]{2,1,0:T(8,128)(2,1)} %get-tuple-element.312, s32[32]{0:T(128)S(1)} %get-tuple-element.311), kind=kOutput, calls=%fused_computation.24.clone.1 | convolution fusion | flops 87818880 | bytes 19923072 | tf_op jit(solution)/shard_map/while/body/eval_jaxpr/kr,kif->rif/dot_general | solution.py:24
  250.8 6.0 %copy.76 = f32[20,128,512]{2,1,0:T(8,128)S(1)} copy(f32[20,128,512]{2,0,1:T(8,128)} %get-tuple-element.104) | data formatting | bytes 10485760 | tf_op jit(solution)/shard_map/while | solution.py:68
  265.0 5.7 %fusion.47 = f32[2048,512]{1,0:T(8,128)} fusion(s32[1024]{0:T(1024)S(1)} %copy-done.16, bf16[1024]{0:T(1024)(128)(2,1)S(1)} %copy-done.18, bf16[128,8,512]{2,1,0:T(8,128)(2,1)} %all-to-all-done.1), kind=kOutput, calls=%fused_computation.55 | convolution fusion | flops 2151677952 | bytes 5249024 | tf_op jit(solution)/shard_map/kr,kif->rif/dot_general | solution.py:24
  270.8 5.8 %fusion.45 = f32[2048,512]{1,0:T(8,128)} fusion(s32[1024]{0:T(1024)S(1)} %copy-done.16, bf16[1024]{0:T(1024)(128)(2,1)S(1)} %copy-done.18, bf16[128,8,512]{2,1,0:T(8,128)(2,1)} %all-to-all-done.1), kind=kOutput, calls=%fused_computation.54 | convolution fusion | flops 2153250816 | bytes 5249024 | tf_op jit(solution)/shard_map/kr,kif->rif/dot_general | solution.py:25
  276.5 140.7 %all-reduce.4.cloned.1.call-done = (f32[512,512]{1,0:T(8,128)}, f32[512,512]{1,0:T(8,128)}) async-done(((f32[512,512]{1,0:T(8,128)}, f32[512,512]{1,0:T(8,128)}), (f32[512,512]{1,0:T(8,128)}, f32[512,512]{1,0:T(8,128)})) %all-reduce.4.cloned.1.call-update) | async-done | bytes 2097168
  419.5 6.6 %fusion.52 = bf16[2048,512]{1,0:T(8,128)(2,1)} fusion(f32[16,128,512]{2,1,0:T(8,128)S(1)} %copy-done.8, f32[2048,512]{1,0:T(8,128)} %fusion.47, f32[2048,512]{1,0:T(8,128)} %fusion.45, f32[2048,512]{1,0:T(8,128)S(1)} %fusion.79, s32[4]{0:T(128)S(1)} %copy-done.14, f32[512,512]{1,0:T(8,128)} %get-tuple-element.207, u32[]{:T(128)S(6)} %multiply.1), kind=kOutput, calls=%fused_computation.59 | convolution fusion | flops 13647872 | bytes 18882580 | tf_op jit(solution)/shard_map/kr,kif->rif/dot_general | solution.py:25
  (101 shorter events, 80.7 us)
Async XLA Ops:
  7.2 150.4 %copy-start = (bf16[512,512]{1,0:T(8,128)(2,1)S(1)}, bf16[512,512]{1,0:T(8,128)(2,1)}, u32[]{:S(2)}) copy-start(bf16[512,512]{1,0:T(8,128)(2,1)} %param.14) | copy-start | bytes 1572868
  14.5 12.0 %copy-start.20 = (s32[96]{0:T(128)S(1)}, s32[96]{0:T(128)}, u32[]{:S(2)}) copy-start(s32[96]{0:T(128)} %param.17) | copy-start | bytes 1156
  14.5 12.1 %copy-start.21 = (s32[96]{0:T(128)S(1)}, s32[96]{0:T(128)}, u32[]{:S(2)}) copy-start(s32[96]{0:T(128)} %param.18) | copy-start | bytes 1156
  14.5 12.2 %copy-start.9 = (bf16[2048,512]{1,0:T(8,128)(2,1)S(1)}, bf16[2048,512]{1,0:T(8,128)(2,1)}, u32[]{:S(2)}) copy-start(bf16[2048,512]{1,0:T(8,128)(2,1)} %param.13) | copy-start | bytes 6291460
  14.5 12.2 %copy-start.13 = (s32[4]{0:T(128)S(1)}, s32[4]{0:T(128)}, u32[]{:S(2)}) copy-start(s32[4]{0:T(128)} %param.19) | copy-start | bytes 52
  14.5 108.8 %all-to-all-start = ((bf16[128,8,512]{2,1,0:T(8,128)(2,1)}), bf16[128,8,512]{2,1,0:T(8,128)(2,1)}, u32[]{:S(2)}, u32[]{:S(2)}) async-start(bf16[128,8,512]{2,1,0:T(8,128)(2,1)} %fusion.69), calls=%async_computation | async-start | bytes 2097152 | tf_op jit(solution)/shard_map/all_to_all | solution.py:97
  73.8 3.2 slice-start
  123.3 2.7 copy-start.4
  150.6 3.4 copy-start.3
  150.6 4.7 %copy-start.7 = (bf16[32,128,512]{2,0,1:T(8,128)(2,1)S(1)}, bf16[32,128,512]{2,0,1:T(8,128)(2,1)}, u32[]{:S(2)}) copy-start(bf16[32,128,512]{2,0,1:T(8,128)(2,1)} %copy.72) | copy-start | bytes 12582916
  157.6 4.2 copy-start.10
  164.3 1.9 copy-start.5
  199.9 65.1 %all-to-all-start.1 = ((bf16[128,8,512]{2,1,0:T(8,128)(2,1)}), bf16[128,8,512]{2,1,0:T(8,128)(2,1)}, u32[]{:S(2)}, u32[]{:S(2)}) async-start(bf16[128,8,512]{2,1,0:T(8,128)(2,1)} %bitcast.126), calls=%async_computation.1 | async-start | bytes 2097152 | tf_op jit(solution)/shard_map/all_to_all | solution.py:147
  204.8 212.5 %all-reduce.4.cloned.1.call-start = ((), (), s32[]{:S(2)}) async-start(), calls=%async_computation.2 | async-start | bytes 4194304
  204.8 1.6 copy-start.6
  250.8 6.0 %copy-start.2 = (f32[20,128,512]{2,0,1:T(8,128)S(1)}, f32[20,128,512]{2,0,1:T(8,128)}, u32[]{:S(2)}) copy-start(f32[20,128,512]{2,0,1:T(8,128)} %get-tuple-element.104) | copy-start | bytes 15728644
  258.3 4.4 %copy-start.11 = (bf16[16,128,512]{2,1,0:T(8,128)(2,1)S(1)}, bf16[16,128,512]{2,1,0:T(8,128)(2,1)}, u32[]{:S(2)}) copy-start(bf16[16,128,512]{2,1,0:T(8,128)(2,1)} %copy-done.10) | copy-start | bytes 6291460
  258.3 4.4 %copy-start.23 = (bf16[2048,512]{1,0:T(8,128)(2,1)S(1)}, bf16[2048,512]{1,0:T(8,128)(2,1)}, u32[]{:S(2)}) copy-start(bf16[2048,512]{1,0:T(8,128)(2,1)} %copy-done.22) | copy-start | bytes 6291460
  262.7 2.3 copy-start.16
  262.7 2.3 copy-start.18
  270.8 146.5 %copy-start.14 = (s32[4]{0:T(128)S(1)}, s32[4]{0:T(128)}, u32[]{:S(2)}) copy-start(s32[4]{0:T(128)} %param.19) | copy-start | bytes 52
  417.3 2.2 copy-start.8
  419.5 6.6 %copy-start.12 = (f32[512,512]{1,0:T(8,128)S(1)}, f32[512,512]{1,0:T(8,128)}, u32[]{:S(2)}) copy-start(f32[512,512]{1,0:T(8,128)} %get-tuple-element.363) | copy-start | bytes 3145732
  419.5 7.6 %copy-start.1 = (bf16[512,512]{1,0:T(8,128)(2,1)S(1)}, bf16[512,512]{1,0:T(8,128)(2,1)}, u32[]{:S(2)}) copy-start(bf16[512,512]{1,0:T(8,128)(2,1)} %param.14) | copy-start | bytes 1572868
  (5 other events, 6.0 us)
Sparse Core Ops, SparseCore 0:
  265.1 152.1 all-reduce.3
where the time goes:
time: 438 us; the launch traced here: 434 us
  matrix products  154 us (35%)
  waiting for transfers between devices  141 us (32%)
  local copies, waits for them, and re-layouts  61.2 us (14%)
  blocking collectives  45.4 us (10%)
  starting transfers between devices  16.9 us (4%)
  between operations  14.8 us (3%)
    unnamed x2, waiting for transfers between devices  141 us
    dot_general x8, matrix products, add_into(): jnp.einsum('kr,kif->rif', selector, upper, preferred_element_type=jnp.flo...  55.5 us
    all_gather x1, blocking collectives, per_device(): hub_all = lax.all_gather(hub_local, 'dom', axis=0, tiled=True)  45.4 us
    dot_general x8, matrix products, add_into(): jnp.einsum('kr,kif->rif', selector, lower, preferred_element_type=jnp.flo...  38.1 us
    dot_general x3, matrix products, spread_advance(): jnp.einsum('kij,kif->kjf', vals_group, picked, preferred_element_type=jnp...  17.3 us
    dot_general x3, matrix products, apply_advance(): jnp.einsum('kij,kjf->kif', vals_group, picked, preferred_element_type=jnp...  17.2 us
    convert_element_type x2, local copies, waits for them, and re-layouts, add_into(): upper = terms.astype(jnp.bfloat16)  15.9 us
    convert_element_type x2, local copies, waits for them, and re-layouts, add_into(): lower = (terms - upper.astype(jnp.float32)).astype(jnp.bfloat16)  15.9 us
  transfers between devices with their start and end apart: 3, of which 1 were waited for; matrix products, arithmetic and copies ran while one was open for 28% of the time, Pallas kernels for 0%

commit v1 on v0

--- a/solution.py
+++ b/solution.py
@@ -82,7 +82,9 @@
     hub_local = jnp.dot(hub_select, features, preferred_element_type=jnp.float32).astype(
         jnp.bfloat16
     )
-    hub_all = lax.all_gather(hub_local, "dom", axis=0, tiled=True)
+    hub_all = jnp.concatenate(
+        lax.all_to_all(jnp.stack([hub_local] * lax.axis_size("dom")), "dom", 0, 0), axis=0
+    )
     targets = send_rows[0]
     counts = send_count[0]
     live_slots = jnp.arange(slot_count, dtype=jnp.int32)[None, :] < counts[:, None]

time: 438 us -> 419 us (0.957)
  blocking collectives: 45.4 us -> 0 us
  starting transfers between devices: 16.9 us -> 31.8 us
    all_gather x1 -> x0, blocking collectives: 45.4 us -> none  [per_device(): hub_all = lax.all_gather(hub_local, 'dom', axis=0, tiled=True)]
    all_to_all x0 -> x1, starting transfers between devices: none -> 11.5 us  [per_device(): lax.all_to_all(jnp.stack([hub_local] * lax.axis_size('dom')), 'dom', 0, 0)]
    all_to_all x1, starting transfers between devices: 4.9 us -> 10.2 us  [per_device(): lax.all_to_all(far_flat.astype(jnp.bfloat16), 'dom', split_axis=0, concat...]
    unnamed x51 -> x44, local copies, waits for them, and re-layouts: 10.9 us -> 9.63 us
  transfers between devices with their start and end apart: 3 -> 4, of which waited for: 1 -> 2; matrix products, arithmetic and copies ran while one was open for 28% -> 32% of each run, Pallas kernels for 0% -> 0%
where the time goes in v1:
time: 419 us; the launch traced here: 414 us
  matrix products  158 us (38%)
  waiting for transfers between devices  141 us (34%)
  local copies, waits for them, and re-layouts  64 us (15%)
  starting transfers between devices  31.8 us (8%)
  between operations  14.8 us (4%)
    unnamed x2, waiting for transfers between devices  141 us
    dot_general x8, matrix products, add_into(): jnp.einsum('kr,kif->rif', selector, upper, preferred_element_type=jnp.flo...  55.5 us
    dot_general x8, matrix products, add_into(): jnp.einsum('kr,kif->rif', selector, lower, preferred_element_type=jnp.flo...  38.2 us
    dot_general x3, matrix products, apply_advance(): jnp.einsum('kij,kjf->kif', vals_group, picked, preferred_element_type=jnp...  18.5 us
    dot_general x3, matrix products, spread_advance(): jnp.einsum('kij,kif->kjf', vals_group, picked, preferred_element_type=jnp...  18.5 us
    convert_element_type x2, local copies, waits for them, and re-layouts, add_into(): upper = terms.astype(jnp.bfloat16)  15.9 us
    convert_element_type x2, local copies, waits for them, and re-layouts, add_into(): lower = (terms - upper.astype(jnp.float32)).astype(jnp.bfloat16)  15.8 us
    dot_general x6, matrix products, pick_blocks(): jnp.einsum('kc,cjf->kjf', selector, blocks, preferred_element_type=jnp.fl...  13 us
  transfers between devices with their start and end apart: 4, of which 2 were waited for; matrix products, arithmetic and copies ran while one was open for 32% of the time, Pallas kernels for 0%

profile of v1, /device:TPU:1, one launch (start us, length us, event | category | flops | bytes accessed | tf_op | source)
XLA Modules:
  0.0 414.0 jit_solution(12666620024827575298)
XLA Ops:
  10.2 11.5 %all-to-all-start = ((bf16[128,4,512]{2,1,0:T(4,128)(2,1)}), bf16[128,4,512]{2,1,0:T(4,128)(2,1)S(1)}, u32[]{:S(2)}, u32[]{:S(2)}) async-start(bf16[128,4,512]{2,1,0:T(4,128)(2,1)} %stack.2), calls=%async_computation | async-start | bytes 1048576 | tf_op jit(solution)/shard_map/all_to_all | solution.py:86
  29.8 4.9 %fusion.69 = bf16[128,8,512]{2,1,0:T(8,128)(2,1)} fusion(bf16[2048,512]{1,0:T(8,128)(2,1)} %param.13, s32[1024]{0:T(1024)S(1)} %eq.165, bf16[1024]{0:T(1024)(128)(2,1)S(1)} %reshape.149), kind=kOutput, calls=%fused_computation.85 | convolution fusion | flops 2152202240 | bytes 3151872 | tf_op jit(solution)/shard_map/dot_general | solution.py:95
  36.1 10.1 %all-to-all-start.1 = ((bf16[128,8,512]{2,1,0:T(8,128)(2,1)}), bf16[128,8,512]{2,1,0:T(8,128)(2,1)}, u32[]{:S(2)}, u32[]{:S(2)}) async-start(bf16[128,8,512]{2,1,0:T(8,128)(2,1)} %fusion.69), calls=%async_computation.1 | async-start | bytes 2097152 | tf_op jit(solution)/shard_map/all_to_all | solution.py:99
  52.2 43.5 %while.6 = (s32[]{:T(128)}, f32[16,128,512]{2,0,1:T(8,128)}, s32[2,32]{1,0:T(2,128)S(1)}, bf16[2,32,128,128]{3,2,1,0:T(8,128)(2,1)S(1)}, s32[2,32]{1,0:T(2,128)S...) while((s32[]{:T(128)}, f32[16,128,512]{2,0,1:T(8,128)}, s32[2,32]{1,0:T(2,128)S(1)}, ...), condition=%wide.region_1.2_spmd.clone, body=%wide.region_0.1_spmd.clone.sunk | while | flops 768607872 | bytes 45614052 | solution.py:46
  59.7 4.9 %fusion.141 = f32[16,128,512]{2,0,1:T(8,128)} fusion(bf16[32,128,512]{2,1,0:T(8,128)(2,1)S(1)} %get-tuple-element.300, s32[32]{0:T(128)S(1)} %get-tuple-element.301), kind=kOutput, calls=%fused_computation.1.clone.1 | convolution fusion | flops 67109376 | bytes 8388736 | tf_op jit(solution)/shard_map/while/body/eval_jaxpr/kr,kif->rif/dot_general | solution.py:25
  64.6 8.6 %select_add_fusion.4 = f32[16,128,512]{2,0,1:T(8,128)} fusion(f32[16,128,512]{2,0,1:T(8,128)} %get-tuple-element.322, f32[16,128,512]{2,0,1:T(8,128)} %fusion.141, bf16[32,128,512]{2,1,0:T(8,128)(2,1)} %get-tuple-element.302, pred[]{:T(512)S(6)} %compare.6, s32[32]{0:T(128)S(1)} %get-tuple-element.301), kind=kOutput, calls=%fused_computation.7.clone.1 | convolution fusion | flops 70255104 | bytes 16777344 | tf_op jit(solution)/shard_map/while/body/eval_jaxpr/kr,kif->rif/dot_general | solution.py:24
  85.5 9.8 %select_add_fusion.4 = f32[16,128,512]{2,0,1:T(8,128)} fusion(f32[16,128,512]{2,0,1:T(8,128)} %get-tuple-element.322, f32[16,128,512]{2,0,1:T(8,128)} %fusion.141, bf16[32,128,512]{2,1,0:T(8,128)(2,1)} %get-tuple-element.302, pred[]{:T(512)S(6)} %compare.6, s32[32]{0:T(128)S(1)} %get-tuple-element.301), kind=kOutput, calls=%fused_computation.7.clone.1 | convolution fusion | flops 70255104 | bytes 16777344 | tf_op jit(solution)/shard_map/while/body/eval_jaxpr/kr,kif->rif/dot_general | solution.py:24
  98.3 10.0 %fusion.43 = (bf16[32,128,512]{1,2,0:T(8,128)(2,1)}, bf16[32,128,512]{1,2,0:T(8,128)(2,1)}) fusion(bf16[96,128,128]{2,1,0:T(8,128)(2,1)} %param.16, bf16[32,128,512]{2,0,1:T(8,128)(2,1)S(1)} %convolution_convert_fusion.3), kind=kOutput, calls=%fused_computation.51 | convolution fusion | flops 545259520 | bytes 13631488 | tf_op jit(solution)/shard_map/while/body/eval_jaxpr/kij,kjf->kif/dot_general | solution.py:36
  108.3 7.9 %copy.71 = bf16[32,128,512]{2,0,1:T(8,128)(2,1)} copy(bf16[32,128,512]{1,2,0:T(8,128)(2,1)} %get-tuple-element.216) | data formatting | bytes 8388608 | tf_op jit(solution)/shard_map/while/body/eval_jaxpr/convert_element_type | solution.py:22
  116.2 7.9 %copy.72 = bf16[32,128,512]{2,0,1:T(8,128)(2,1)} copy(bf16[32,128,512]{1,2,0:T(8,128)(2,1)} %get-tuple-element.215) | data formatting | bytes 8388608 | tf_op jit(solution)/shard_map/while/body/eval_jaxpr/convert_element_type | solution.py:23
  139.4 10.1 %fusion.42 = (bf16[32,128,512]{1,2,0:T(8,128)(2,1)}, bf16[32,128,512]{1,2,0:T(8,128)(2,1)}) fusion(bf16[96,128,128]{2,1,0:T(8,128)(2,1)} %param.16, bf16[32,128,512]{2,0,1:T(8,128)(2,1)S(1)} %convolution_convert_fusion.4), kind=kOutput, calls=%fused_computation.48 | convolution fusion | flops 545259520 | bytes 13631488 | tf_op jit(solution)/shard_map/while/body/eval_jaxpr/kij,kif->kjf/dot_general | solution.py:58
  149.5 7.9 %copy.79 = bf16[32,128,512]{2,0,1:T(8,128)(2,1)} copy(bf16[32,128,512]{1,2,0:T(8,128)(2,1)} %get-tuple-element.214) | data formatting | bytes 8388608 | tf_op jit(solution)/shard_map/while/body/eval_jaxpr/convert_element_type | solution.py:22
  161.6 7.9 %copy.80 = bf16[32,128,512]{2,0,1:T(8,128)(2,1)} copy(bf16[32,128,512]{1,2,0:T(8,128)(2,1)} %get-tuple-element.213) | data formatting | bytes 8388608 | tf_op jit(solution)/shard_map/while/body/eval_jaxpr/convert_element_type | solution.py:23
  174.3 10.2 %all-to-all-start.2 = ((bf16[128,8,512]{2,1,0:T(8,128)(2,1)}), bf16[128,8,512]{2,1,0:T(8,128)(2,1)}, u32[]{:S(2)}, u32[]{:S(2)}) async-start(bf16[128,8,512]{2,1,0:T(8,128)(2,1)} %bitcast.123), calls=%async_computation.2 | async-start | bytes 2097152 | tf_op jit(solution)/shard_map/all_to_all | solution.py:149
  184.6 45.9 %while.7 = (s32[]{:T(128)}, f32[20,128,512]{2,0,1:T(8,128)}, s32[2,32]{1,0:T(2,128)S(1)}, bf16[2,32,128,128]{2,3,1,0:T(8,128)(2,1)}, s32[2,32]{1,0:T(2,128)S(1)}...) while((s32[]{:T(128)}, f32[20,128,512]{2,0,1:T(8,128)}, s32[2,32]{1,0:T(2,128)S(1)}, ...), condition=%wide.region_3.4_spmd.clone, body=%wide.region_2.3_spmd.clone.sunk | while | flops 786171648 | bytes 57672704 | solution.py:68
  190.4 5.8 %fusion.149 = f32[20,128,512]{2,0,1:T(8,128)} fusion(bf16[32,128,512]{2,1,0:T(8,128)(2,1)S(1)} %get-tuple-element.310, s32[32]{0:T(128)S(1)} %get-tuple-element.311), kind=kOutput, calls=%fused_computation.25.clone.1 | convolution fusion | flops 83886720 | bytes 9437312 | tf_op jit(solution)/shard_map/while/body/eval_jaxpr/kr,kif->rif/dot_general | solution.py:25
  196.2 10.3 %select_add_fusion.5 = f32[20,128,512]{2,0,1:T(8,128)} fusion(f32[20,128,512]{2,0,1:T(8,128)} %get-tuple-element.346, f32[20,128,512]{2,0,1:T(8,128)} %fusion.149, pred[]{:T(512)S(6)} %compare.7, bf16[32,128,512]{2,1,0:T(8,128)(2,1)} %get-tuple-element.312, s32[32]{0:T(128)S(1)} %get-tuple-element.311), kind=kOutput, calls=%fused_computation.24.clone.1 | convolution fusion | flops 87818880 | bytes 19923072 | tf_op jit(solution)/shard_map/while/body/eval_jaxpr/kr,kif->rif/dot_general | solution.py:24
  212.4 5.8 %fusion.149 = f32[20,128,512]{2,0,1:T(8,128)} fusion(bf16[32,128,512]{2,1,0:T(8,128)(2,1)S(1)} %get-tuple-element.310, s32[32]{0:T(128)S(1)} %get-tuple-element.311), kind=kOutput, calls=%fused_computation.25.clone.1 | convolution fusion | flops 83886720 | bytes 9437312 | tf_op jit(solution)/shard_map/while/body/eval_jaxpr/kr,kif->rif/dot_general | solution.py:25
  218.1 12.1 %select_add_fusion.5 = f32[20,128,512]{2,0,1:T(8,128)} fusion(f32[20,128,512]{2,0,1:T(8,128)} %get-tuple-element.346, f32[20,128,512]{2,0,1:T(8,128)} %fusion.149, pred[]{:T(512)S(6)} %compare.7, bf16[32,128,512]{2,1,0:T(8,128)(2,1)} %get-tuple-element.312, s32[32]{0:T(128)S(1)} %get-tuple-element.311), kind=kOutput, calls=%fused_computation.24.clone.1 | convolution fusion | flops 87818880 | bytes 19923072 | tf_op jit(solution)/shard_map/while/body/eval_jaxpr/kr,kif->rif/dot_general | solution.py:24
  230.5 6.0 %copy.76 = f32[20,128,512]{2,1,0:T(8,128)S(1)} copy(f32[20,128,512]{2,0,1:T(8,128)} %get-tuple-element.104) | data formatting | bytes 10485760 | tf_op jit(solution)/shard_map/while | solution.py:68
  244.7 5.7 %fusion.47 = f32[2048,512]{1,0:T(8,128)} fusion(s32[1024]{0:T(1024)S(1)} %copy-done.13, bf16[1024]{0:T(1024)(128)(2,1)S(1)} %copy-done.15, bf16[128,8,512]{2,1,0:T(8,128)(2,1)} %all-to-all-done.2), kind=kOutput, calls=%fused_computation.55 | convolution fusion | flops 2151677952 | bytes 5249024 | tf_op jit(solution)/shard_map/kr,kif->rif/dot_general | solution.py:24
  250.5 5.8 %fusion.45 = f32[2048,512]{1,0:T(8,128)} fusion(s32[1024]{0:T(1024)S(1)} %copy-done.13, bf16[1024]{0:T(1024)(128)(2,1)S(1)} %copy-done.15, bf16[128,8,512]{2,1,0:T(8,128)(2,1)} %all-to-all-done.2), kind=kOutput, calls=%fused_computation.54 | convolution fusion | flops 2153250816 | bytes 5249024 | tf_op jit(solution)/shard_map/kr,kif->rif/dot_general | solution.py:25
  256.2 140.7 %all-reduce.4.cloned.1.call-done = (f32[512,512]{1,0:T(8,128)}, f32[512,512]{1,0:T(8,128)}) async-done(((f32[512,512]{1,0:T(8,128)}, f32[512,512]{1,0:T(8,128)}), (f32[512,512]{1,0:T(8,128)}, f32[512,512]{1,0:T(8,128)})) %all-reduce.4.cloned.1.call-update) | async-done | bytes 2097168
  399.1 6.6 %fusion.52 = bf16[2048,512]{1,0:T(8,128)(2,1)} fusion(f32[16,128,512]{2,1,0:T(8,128)S(1)} %copy-done.6, f32[2048,512]{1,0:T(8,128)} %fusion.47, f32[2048,512]{1,0:T(8,128)} %fusion.45, f32[2048,512]{1,0:T(8,128)S(1)} %fusion.78, s32[4]{0:T(128)S(1)} %copy-done.11, f32[512,512]{1,0:T(8,128)} %get-tuple-element.207, u32[]{:T(128)S(6)} %multiply.1), kind=kOutput, calls=%fused_computation.59 | convolution fusion | flops 13647872 | bytes 18882580 | tf_op jit(solution)/shard_map/kr,kif->rif/dot_general | solution.py:25
  (96 shorter events, 88.0 us)
Async XLA Ops:
  7.2 123.9 %copy-start = (bf16[512,512]{1,0:T(8,128)(2,1)S(1)}, bf16[512,512]{1,0:T(8,128)(2,1)}, u32[]{:S(2)}) copy-start(bf16[512,512]{1,0:T(8,128)(2,1)} %param.14) | copy-start | bytes 1572868
  7.2 19.6 %copy-start.18 = (s32[96]{0:T(128)S(1)}, s32[96]{0:T(128)}, u32[]{:S(2)}) copy-start(s32[96]{0:T(128)} %param.18) | copy-start | bytes 1156
  7.2 19.5 %copy-start.17 = (s32[96]{0:T(128)S(1)}, s32[96]{0:T(128)}, u32[]{:S(2)}) copy-start(s32[96]{0:T(128)} %param.17) | copy-start | bytes 1156
  10.2 25.0 %all-to-all-start = ((bf16[128,4,512]{2,1,0:T(4,128)(2,1)}), bf16[128,4,512]{2,1,0:T(4,128)(2,1)S(1)}, u32[]{:S(2)}, u32[]{:S(2)}) async-start(bf16[128,4,512]{2,1,0:T(4,128)(2,1)} %stack.2), calls=%async_computation | async-start | bytes 1048576 | tf_op jit(solution)/shard_map/all_to_all | solution.py:86
  22.6 7.1 %copy-start.12 = (s32[1024]{0:T(1024)}, s32[1024]{0:T(1024)S(1)}, u32[]{:S(2)}) copy-start(s32[1024]{0:T(1024)S(1)} %eq.165) | copy-start | bytes 12292
  23.5 6.2 %copy-start.14 = (bf16[1024]{0:T(1024)(128)(2,1)}, bf16[1024]{0:T(1024)(128)(2,1)S(1)}, u32[]{:S(2)}) copy-start(bf16[1024]{0:T(1024)(128)(2,1)S(1)} %reshape.149) | copy-start | bytes 6148
  36.1 59.7 %all-to-all-start.1 = ((bf16[128,8,512]{2,1,0:T(8,128)(2,1)}), bf16[128,8,512]{2,1,0:T(8,128)(2,1)}, u32[]{:S(2)}, u32[]{:S(2)}) async-start(bf16[128,8,512]{2,1,0:T(8,128)(2,1)} %fusion.69), calls=%async_computation.1 | async-start | bytes 2097152 | tf_op jit(solution)/shard_map/all_to_all | solution.py:99
  124.1 3.4 copy-start.3
  124.1 4.7 %copy-start.5 = (bf16[32,128,512]{2,0,1:T(8,128)(2,1)S(1)}, bf16[32,128,512]{2,0,1:T(8,128)(2,1)}, u32[]{:S(2)}) copy-start(bf16[32,128,512]{2,0,1:T(8,128)(2,1)} %copy.72) | copy-start | bytes 12582916
  129.9 1.6 copy-start.16
  131.1 4.2 %copy-start.7 = (bf16[16,128,512]{2,1,0:T(8,128)(2,1)}, bf16[16,128,512]{2,1,0:T(8,128)(2,1)S(1)}, u32[]{:S(2)}) copy-start(bf16[16,128,512]{2,1,0:T(8,128)(2,1)S(1)} %copy.73) | copy-start | bytes 6291460
  174.3 70.4 %all-to-all-start.2 = ((bf16[128,8,512]{2,1,0:T(8,128)(2,1)}), bf16[128,8,512]{2,1,0:T(8,128)(2,1)}, u32[]{:S(2)}, u32[]{:S(2)}) async-start(bf16[128,8,512]{2,1,0:T(8,128)(2,1)} %bitcast.123), calls=%async_computation.2 | async-start | bytes 2097152 | tf_op jit(solution)/shard_map/all_to_all | solution.py:149
  184.6 212.4 %all-reduce.4.cloned.1.call-start = ((), (), s32[]{:S(2)}) async-start(), calls=%async_computation.3 | async-start | bytes 4194304
  184.6 1.6 copy-start.4
  206.6 1.6 copy-start.4
  230.5 6.0 %copy-start.2 = (f32[20,128,512]{2,0,1:T(8,128)S(1)}, f32[20,128,512]{2,0,1:T(8,128)}, u32[]{:S(2)}) copy-start(f32[20,128,512]{2,0,1:T(8,128)} %get-tuple-element.104) | copy-start | bytes 15728644
  238.0 4.4 %copy-start.8 = (bf16[16,128,512]{2,1,0:T(8,128)(2,1)S(1)}, bf16[16,128,512]{2,1,0:T(8,128)(2,1)}, u32[]{:S(2)}) copy-start(bf16[16,128,512]{2,1,0:T(8,128)(2,1)} %copy-done.7) | copy-start | bytes 6291460
  238.0 4.4 %copy-start.20 = (bf16[2048,512]{1,0:T(8,128)(2,1)S(1)}, bf16[2048,512]{1,0:T(8,128)(2,1)}, u32[]{:S(2)}) copy-start(bf16[2048,512]{1,0:T(8,128)(2,1)} %copy-done.19) | copy-start | bytes 6291460
  242.4 2.3 copy-start.13
  242.4 2.3 copy-start.15
  250.5 146.5 %copy-start.11 = (s32[4]{0:T(128)S(1)}, s32[4]{0:T(128)}, u32[]{:S(2)}) copy-start(s32[4]{0:T(128)} %param.19) | copy-start | bytes 52
  396.9 2.2 copy-start.6
  399.1 6.6 %copy-start.10 = (f32[512,512]{1,0:T(8,128)S(1)}, f32[512,512]{1,0:T(8,128)}, u32[]{:S(2)}) copy-start(f32[512,512]{1,0:T(8,128)} %get-tuple-element.363) | copy-start | bytes 3145732
  399.1 7.6 %copy-start.1 = (bf16[512,512]{1,0:T(8,128)(2,1)S(1)}, bf16[512,512]{1,0:T(8,128)(2,1)}, u32[]{:S(2)}) copy-start(bf16[512,512]{1,0:T(8,128)(2,1)} %param.14) | copy-start | bytes 1572868
  (2 other events, 2.2 us)
Sparse Core Ops, SparseCore 0:
  244.8 152.0 all-reduce.3
